TPU v7x, 32 devices: a whole 2x2x4 slice. The times are simulated.
32 devices in a mesh: front: 8 (over z, core), tile: 4 (over y, x).
Axes of the slice: x: 2, y: 2, z: 4, core: 2. Of those that a mesh axis runs over, the one named last changes fastest.
Arguments:
- child_rhs: float32 [8, 2048, 256], P('front', 'tile'), may hold values from -6 to 6
- child_lower: float32 [8, 2048, 2048], P('front', 'tile'), as said below
- child_border: float32 [8, 2048, 2048], P('front', 'tile'), may hold values from -0.125 to 0.125
- child_upper_border: float32 [8, 2048, 2048], P('front', 'tile'), may hold values from -0.125 to 0.125
- child_upper: float32 [8, 2048, 2048], P('front', 'tile'), as said below
- parent_rhs: float32 [8, 512, 256], P('front', 'tile'), may hold values from -6 to 6
- parent_lower: float32 [8, 512, 2048], P('front', 'tile'), as said below
- parent_upper: float32 [8, 512, 2048], P('front', 'tile'), as said below
- border_map: int32 [8, 2048], P('front'), may hold values from 0 to 2047, as said below
- border_count: int32 [8], P('front'), may hold values from 512 to 2048, as said below
Outputs:
- child_solution: float32 [8, 2048, 256], P('front', 'tile')
- parent_solution: float32 [8, 512, 256], P('front', 'tile')
Inputs may be any that keep to these rules, and one draw needn't show every extreme that they name: `border_map`: within one child the 2048 entries are distinct parent rows. Group g of parent rows holds the rows m with (m mod (512)) // 128 = g, for g below 4. In every aligned block of 512 border rows of a child, each group receives either no row or exactly 256 rows, and each group receives 2048 // 4 border rows of the child in all. `border_count`: some child has all 2048 border rows live. `child_lower`: lower triangular including the diagonal. `child_upper`: upper triangular including the diagonal. `parent_lower`: each parent's 2048 rows form a lower triangular matrix including the diagonal. `parent_upper`: each parent's 2048 rows form an upper triangular matrix including the diagonal.
All inputs are finite; a program needn't handle non-finite values.
Results may differ from a plain program's by a relative error of at most 0.00013.
Values sent between devices are 32-bit elements; how exact they have to be, the bound alone decides.
A program may use at most 64 MiB of HBM per device.

v0:
```python
import jax
import jax.numpy as jnp
from jax import lax
from jax.sharding import PartitionSpec as P


def partner_2(block, axis, apart):
    count = lax.axis_size(axis)
    route = []
    for low in range(count):
        high = low | 1 << apart
        if high != low and high < count:
            route += [(low, high), (high, low)]
    return lax.ppermute(block, axis, route)


def product(matrix, vector):
    return jnp.dot(
        matrix, vector, preferred_element_type=jnp.float32, precision=lax.Precision.HIGHEST
    )


def apply_rows(matrix, local_rows):
    return product(matrix, lax.all_gather(local_rows, "tile", axis=0, tiled=True))


def pair_quarters(stacked, quarter):
    for bit_number in (0, 1):
        partner = partner_2(stacked, "front", bit_number)
        upper_bit = jnp.right_shift(quarter, bit_number) % 2
        stacked = jnp.where(
            upper_bit == 0,
            jnp.concatenate([stacked, partner], 0),
            jnp.concatenate([partner, stacked], 0),
        )
    return stacked


def assemble(block, quarter):
    whole_quarter = lax.all_gather(block, "tile", axis=0, tiled=True)
    stacked = pair_quarters(whole_quarter[None], quarter)
    return stacked.reshape(-1, block.shape[1])


def layout_index(parent_row, quarter_rows, slab_rows):
    return (
        parent_row % quarter_rows // slab_rows * (4 * slab_rows)
        + parent_row // quarter_rows * slab_rows
        + parent_row % slab_rows
    )


def local(
    child_rhs,
    child_lower,
    child_border,
    child_upper_border,
    child_upper,
    parent_rhs,
    parent_lower,
    parent_upper,
    border_map,
    border_count,
):
    tile_pos = lax.axis_index("tile")
    quarter = lax.axis_index("front") % 4
    border_rows = child_border.shape[1]
    slab_rows = parent_lower.shape[1]
    parent_rows = parent_lower.shape[2]
    quarter_rows = parent_rows // 4
    slab_width = 4 * slab_rows
    live_total = border_count[0]
    map_whole = border_map[0]
    forward_child = apply_rows(child_lower[0], child_rhs[0])
    own_ids = tile_pos * border_rows + jnp.arange(border_rows, dtype=jnp.int32)
    own_map = lax.dynamic_slice_in_dim(map_whole, tile_pos * border_rows, border_rows, 0)
    alive_rows = own_ids < live_total
    update = -apply_rows(child_border[0], forward_child)
    update = jnp.where(alive_rows[:, None], update, 0.0)
    target = layout_index(own_map, quarter_rows, slab_rows)
    target = jnp.where(alive_rows, target, -1)
    row_ids = jnp.arange(slab_width * lax.axis_size("tile"), dtype=jnp.int32)
    selector = (row_ids[:, None] == target[None, :]).astype(jnp.float32)
    scattered = lax.psum_scatter(product(selector, update), "tile", scatter_dimension=0, tiled=True)
    stacked = scattered.reshape(4, slab_rows, scattered.shape[1])
    for bit_number in (1, 0):
        half_size = stacked.shape[0] // 2
        upper_bit = jnp.right_shift(quarter, bit_number) % 2
        retained = lax.dynamic_slice_in_dim(stacked, upper_bit * half_size, half_size, 0)
        sending = lax.dynamic_slice_in_dim(stacked, (1 - upper_bit) * half_size, half_size, 0)
        stacked = retained + partner_2(sending, "front", bit_number)
    gathered = stacked[0]
    right_parent = parent_rhs[0] + gathered
    forward_parent = product(parent_lower[0], assemble(right_parent, quarter))
    solved_parent = product(parent_upper[0], assemble(forward_parent, quarter))
    parent_whole = assemble(solved_parent, quarter)
    selector = (
        (own_map[:, None] == jnp.arange(parent_rows, dtype=jnp.int32)[None, :])
        & alive_rows[:, None]
    ).astype(jnp.float32)
    border_values = product(selector, parent_whole)
    reduced = forward_child - apply_rows(child_upper_border[0], border_values)
    child_solution = apply_rows(child_upper[0], reduced)
    return (child_solution[None], solved_parent[None])


def solution(mesh):
    return jax.shard_map(
        local,
        mesh=mesh,
        in_specs=(
            P("front", "tile", None),
            P("front", "tile", None),
            P("front", "tile", None),
            P("front", "tile", None),
            P("front", "tile", None),
            P("front", "tile", None),
            P("front", "tile", None),
            P("front", "tile", None),
            P("front", None),
            P("front"),
        ),
        out_specs=(P("front", "tile", None), P("front", "tile", None)),
        check_vma=False,
    )
```

profile of v0, /device:TPU:0, one launch (start us, length us, event | category | flops | bytes accessed | tf_op | source)
XLA Modules:
  0.0 388.4 jit_solution(4923493146791884085)
XLA Ops:
  7.2 0.7 all-gather.13.cloned.1.call-update
  8.0 39.9 %all-gather.13.cloned.1.call-done = f32[1,2048,256]{2,1,0:T(8,128)} async-done(((f32[1,512,256]{2,1,0:T(8,128)}), f32[1,2048,256]{2,1,0:T(8,128)}) %all-gather.13.cloned.1.call-update) | async-done | bytes 2097168 | tf_op jit(solution)/shard_map/all_gather | solution.py:24
  47.9 7.1 %fusion.6 = f32[512,256]{1,0:T(8,128)} fusion(f32[1,512,2048]{2,1,0:T(8,128)} %param.11, f32[1,2048,256]{2,1,0:T(8,128)} %all-gather.13.cloned.1.call-done), kind=kOutput, calls=%fused_computation.6 | convolution fusion | flops 3221225472 | bytes 6815744 | tf_op jit(solution)/shard_map/dot_general | solution.py:18
  55.0 0.0 reduce-scatter.2.cloned.1.call-start
  55.7 0.7 compare_select_fusion
  56.5 34.0 %all-gather.7.cloned.1.call-done = f32[2048,256]{1,0:T(8,128)} async-done(((f32[512,256]{1,0:T(8,128)}), f32[2048,256]{1,0:T(8,128)}) %all-gather.7.cloned.1.call-update) | async-done | bytes 2097168 | tf_op jit(solution)/shard_map/all_gather | solution.py:24
  90.5 9.3 %fusion.19 = f32[256,512]{1,0:T(8,128)S(1)} fusion(f32[2048,256]{1,0:T(8,128)} %all-gather.7.cloned.1.call-done, f32[1,512,2048]{2,1,0:T(8,128)} %param.12, pred[512]{0:T(512)(128)(4,1)S(1)} %add_compare_fusion), kind=kOutput, calls=%fused_computation.21 | convolution fusion | flops 3221487616 | bytes 6816256 | tf_op jit(solution)/shard_map/dot_general | solution.py:18
  99.8 3.3 fusion.11
  103.2 35.3 %reduce-scatter.2.cloned.1.call-done = f32[512,256]{1,0:T(8,128)} async-done(((f32[2048,256]{1,0:T(8,128)}), f32[512,256]{1,0:T(8,128)}) %reduce-scatter.2.cloned.1.call-update) | async-done | bytes 524304 | tf_op jit(solution)/shard_map/reduce_scatter | solution.py:84
  138.5 1.1 constant_dynamic-slice_fusion.1
  139.6 0.1 copy.26
  139.7 1.6 collective-permute-start
  141.2 0.1 copy.25
  141.4 6.4 %collective-permute-done = f32[2,128,256]{1,2,0:T(8,128)S(1)} collective-permute-done((f32[2,128,256]{1,2,0:T(8,128)S(1)}, f32[2,128,256]{1,2,0:T(8,128)S(1)}, u32[]{:S(2)}, u32[]{:S(2)}) %collective-permute-start) | collective-permute-done | bytes 262176 | tf_op jit(solution)/shard_map/ppermute | solution.py:14
  147.9 0.1 collective-permute-start.1
  148.0 0.1 copy.19
  148.1 1.2 collective-permute-done.1
  149.3 14.2 %all-gather.1 = f32[1,512,256]{1,2,0:T(8,128)S(1)} all-gather(f32[1,128,256]{1,2,0:T(8,128)S(1)} %add_add_fusion), channel_id=3, replica_groups=mesh['front'=8,'tile'=4] {'tile'}, dimensions={1}, use_global_device_ids=true | all-gather | bytes 655360 | tf_op jit(solution)/shard_map/all_gather | solution.py:40
  163.5 1.9 collective-permute-done.2
  165.5 0.1 maximum_select_fusion.3
  165.6 1.6 collective-permute-start.3
  167.1 23.8 %collective-permute-done.3 = f32[2,512,256]{1,2,0:T(8,128)} collective-permute-done((f32[2,512,256]{1,2,0:T(8,128)S(1)}, f32[2,512,256]{1,2,0:T(8,128)}, u32[]{:S(2)}, u32[]{:S(2)}) %collective-permute-start.3) | collective-permute-done | bytes 1048608 | tf_op jit(solution)/shard_map/ppermute | solution.py:14
  191.0 2.7 maximum_select_fusion
  193.6 1.8 copy.20
  195.5 5.0 %convolution_bitcast_fusion = f32[128,256]{0,1:T(8,128)S(1)} fusion(f32[2048,256]{1,0:T(8,128)} %bitcast.62, f32[1,128,2048]{2,1,0:T(8,128)S(1)} %copy-done), kind=kOutput, calls=%fused_computation.25 | convolution fusion | flops 805306368 | bytes 3276800 | tf_op jit(solution)/shard_map/dot_general | solution.py:18
  200.5 11.5 %all_gather.24 = f32[512,256]{0,1:T(8,128)S(1)} all-gather(f32[128,256]{0,1:T(8,128)S(1)} %convolution_bitcast_fusion), channel_id=1, replica_groups=mesh['front'=8,'tile'=4] {'tile'}, dimensions={0}, use_global_device_ids=true | all-gather | bytes 655360 | tf_op jit(solution)/shard_map/all_gather | solution.py:40
  212.0 1.9 collective-permute-done.4
  213.9 0.1 maximum_select_fusion.4
  214.1 1.6 collective-permute-start.5
  215.6 23.7 %collective-permute-done.5 = f32[2,512,256]{1,2,0:T(8,128)S(1)} collective-permute-done((f32[2,512,256]{1,2,0:T(8,128)S(1)}, f32[2,512,256]{1,2,0:T(8,128)S(1)}, u32[]{:S(2)}, u32[]{:S(2)}) %collective-permute-start.5) | collective-permute-done | bytes 1048608 | tf_op jit(solution)/shard_map/ppermute | solution.py:14
  239.3 0.2 maximum_select_fusion.1
  239.6 1.8 copy.21
  241.4 5.3 %fusion.31 = f32[256,128]{1,0:T(8,128)S(1)} fusion(f32[2048,256]{1,0:T(8,128)} %bitcast.63, f32[1,128,2048]{2,1,0:T(8,128)} %param.17), kind=kOutput, calls=%fused_computation.29 | convolution fusion | flops 805306368 | bytes 3276800 | tf_op jit(solution)/shard_map/dot_general | solution.py:18
  246.7 12.5 %all_gather.25 = f32[512,256]{0,1:T(8,128)S(1)} all-gather(f32[128,256]{0,1:T(8,128)S(1)} %bitcast.69), channel_id=1, replica_groups=mesh['front'=8,'tile'=4] {'tile'}, dimensions={0}, use_global_device_ids=true | all-gather | bytes 655360 | tf_op jit(solution)/shard_map/all_gather | solution.py:40
  259.2 1.9 collective-permute-done.6
  261.1 0.1 maximum_select_fusion.5
  261.2 1.6 collective-permute-start.7
  262.8 23.7 %collective-permute-done.7 = f32[2,512,256]{1,2,0:T(8,128)S(1)} collective-permute-done((f32[2,512,256]{1,2,0:T(8,128)S(1)}, f32[2,512,256]{1,2,0:T(8,128)S(1)}, u32[]{:S(2)}, u32[]{:S(2)}) %collective-permute-start.7) | collective-permute-done | bytes 1048608 | tf_op jit(solution)/shard_map/ppermute | solution.py:14
  286.5 0.2 maximum_select_fusion.2
  286.8 1.8 copy.22
  288.6 4.9 %fusion.9 = f32[512,256]{1,0:T(8,128)} fusion(f32[2048,256]{1,0:T(8,128)} %bitcast.68, s32[512]{0:T(512)S(1)} %bitcast.72, pred[512]{0:T(512)(128)(4,1)S(1)} %add_compare_fusion), kind=kOutput, calls=%fused_computation.11 | convolution fusion | flops 3223322624 | bytes 2624000 | tf_op jit(solution)/shard_map/dot_general | solution.py:18
  293.5 0.0 all-gather.11.cloned.1.call-start
  293.5 35.4 %all-gather.9.cloned.1.call-done = f32[2048,256]{1,0:T(8,128)} async-done(((f32[512,256]{1,0:T(8,128)}), f32[2048,256]{1,0:T(8,128)}) %all-gather.9.cloned.1.call-update) | async-done | bytes 2097168 | tf_op jit(solution)/shard_map/all_gather | solution.py:24
  329.0 7.1 %fusion.28 = f32[512,256]{1,0:T(8,128)} fusion(f32[512,256]{1,0:T(8,128)S(1)} %copy-done.1, f32[2048,256]{1,0:T(8,128)} %all-gather.9.cloned.1.call-done, f32[1,512,2048]{2,1,0:T(8,128)} %param.13), kind=kOutput, calls=%fused_computation.24 | convolution fusion | flops 3221356544 | bytes 7340032 | tf_op jit(solution)/shard_map/dot_general | solution.py:18
  336.1 0.8 copy.24
  336.9 34.7 %all-gather.11.cloned.1.call-done = f32[2048,256]{1,0:T(8,128)} async-done(((f32[512,256]{1,0:T(8,128)}), f32[2048,256]{1,0:T(8,128)}) %all-gather.11.cloned.1.call-update) | async-done | bytes 2097168 | tf_op jit(solution)/shard_map/all_gather | solution.py:24
  371.6 9.3 %fusion.25 = f32[1,512,256]{1,2,0:T(8,128)S(1)} fusion(f32[2048,256]{1,0:T(8,128)} %all-gather.11.cloned.1.call-done, f32[1,512,2048]{2,1,0:T(8,128)} %param.14), kind=kOutput, calls=%fused_computation.23 | convolution fusion | flops 3221225472 | bytes 6815744 | tf_op jit(solution)/shard_map/dot_general | solution.py:18
  380.9 1.0 copy.23
  (22 shorter events, 0.3 us)
Async XLA Ops:
  7.2 188.3 %copy-start = (f32[1,128,2048]{2,1,0:T(8,128)S(1)}, f32[1,128,2048]{2,1,0:T(8,128)}, u32[]{:S(2)}) copy-start(f32[1,128,2048]{2,1,0:T(8,128)} %param.16) | copy-start | bytes 3145732
  7.2 40.7 %all-gather.13.cloned.1.call-start = ((), (), s32[]{:S(2)}) async-start(), calls=%async_computation.5 | async-start | bytes 2621440 | tf_op jit(solution)/shard_map/all_gather | solution.py:24
  7.9 82.6 %all-gather.7.cloned.1.call-start = ((), (), s32[]{:S(2)}) async-start(), calls=%async_computation.1 | async-start | bytes 2621440 | tf_op jit(solution)/shard_map/all_gather | solution.py:24
  55.0 83.5 %reduce-scatter.2.cloned.1.call-start = ((), (), s32[]{:S(2)}) async-start(), calls=%async_computation.2 | async-start | bytes 2621440 | tf_op jit(solution)/shard_map/reduce_scatter | solution.py:84
  103.1 44.8 %copy-start.3 = (f32[1,128,256]{2,1,0:T(8,128)S(1)}, f32[1,128,256]{2,1,0:T(8,128)}, u32[]{:S(2)}) copy-start(f32[1,128,256]{2,1,0:T(8,128)} %param.15) | copy-start | bytes 393220
  103.1 225.8 %all-gather.9.cloned.1.call-start = ((), (), s32[]{:S(2)}) async-start(), calls=%async_computation.3 | async-start | bytes 2621440 | tf_op jit(solution)/shard_map/all_gather | solution.py:24
  139.7 8.1 %collective-permute-start = (f32[2,128,256]{1,2,0:T(8,128)S(1)}, f32[2,128,256]{1,2,0:T(8,128)S(1)}, u32[]{:S(2)}, u32[]{:S(2)}) collective-permute-start(f32[2,128,256]{1,2,0:T(8,128)S(1)} %copy.26), channel_id=1, source_target_pairs={{0,8},{8,0},{4,12},{12,4},{16,24},{24,16},{20,28},{28,20},{1,9},{9... | collective-permute-start | bytes 786440 | tf_op jit(solution)/shard_map/ppermute | solution.py:14
  147.9 1.4 collective-permute-start.1
  163.5 1.9 collective-permute-start.2
  165.6 1.6 copy-start.2
  165.6 25.4 %collective-permute-start.3 = (f32[2,512,256]{1,2,0:T(8,128)S(1)}, f32[2,512,256]{1,2,0:T(8,128)}, u32[]{:S(2)}, u32[]{:S(2)}) collective-permute-start(f32[2,512,256]{1,2,0:T(8,128)S(1)} %maximum_select_fusion.3), channel_id=1, source_target_pairs={{0,8},{8,0},{4,12},{12,4},{16,24},{24,16},{20,28},{28,20},{1,9},{9... | collective-permute-start | bytes 3145736 | tf_op jit(solution)/shard_map/ppermute | solution.py:14
  212.0 1.9 collective-permute-start.4
  214.1 25.3 %collective-permute-start.5 = (f32[2,512,256]{1,2,0:T(8,128)S(1)}, f32[2,512,256]{1,2,0:T(8,128)S(1)}, u32[]{:S(2)}, u32[]{:S(2)}) collective-permute-start(f32[2,512,256]{1,2,0:T(8,128)S(1)} %maximum_select_fusion.4), channel_id=1, source_target_pairs={{0,8},{8,0},{4,12},{12,4},{16,24},{24,16},{20,28},{28,20},{1,9},{9... | collective-permute-start | bytes 3145736 | tf_op jit(solution)/shard_map/ppermute | solution.py:14
  259.2 1.9 collective-permute-start.6
  261.2 25.3 %collective-permute-start.7 = (f32[2,512,256]{1,2,0:T(8,128)S(1)}, f32[2,512,256]{1,2,0:T(8,128)S(1)}, u32[]{:S(2)}, u32[]{:S(2)}) collective-permute-start(f32[2,512,256]{1,2,0:T(8,128)S(1)} %maximum_select_fusion.5), channel_id=1, source_target_pairs={{0,8},{8,0},{4,12},{12,4},{16,24},{24,16},{20,28},{28,20},{1,9},{9... | collective-permute-start | bytes 3145736 | tf_op jit(solution)/shard_map/ppermute | solution.py:14
  288.6 40.4 %copy-start.1 = (f32[512,256]{1,0:T(8,128)S(1)}, f32[512,256]{1,0:T(8,128)}, u32[]{:S(2)}) copy-start(f32[512,256]{1,0:T(8,128)} %fusion.6) | copy-start | bytes 1572868
  293.5 78.1 %all-gather.11.cloned.1.call-start = ((), (), s32[]{:S(2)}) async-start(), calls=%async_computation.4 | async-start | bytes 2621440 | tf_op jit(solution)/shard_map/all_gather | solution.py:24
Sparse Core Ops, SparseCore 0:
  9.9 38.0 all-gather.12
  55.1 35.3 all-gather.6
  103.3 35.1 reduce-scatter.1
  293.6 35.3 all-gather.8
  336.2 35.3 all-gather.10
where the time goes:
time: 389 us; the launch traced here: 388 us
  waiting for transfers between devices  265 us (68%)
  matrix products  51.3 us (13%)
  blocking collectives  38.3 us (10%)
  between operations  14.7 us (4%)
  local copies, waits for them, and re-layouts  8.67 us (2%)
  starting transfers between devices  6.48 us (2%)
  other arithmetic  4.29 us (1%)
    all_gather x4, waiting for transfers between devices, apply_rows(): lax.all_gather(local_rows, 'tile', axis=0, tiled=True)  144 us
    ppermute x8, waiting for transfers between devices, partner_2(): return lax.ppermute(block, axis, route)  84.6 us
    dot_general x8, matrix products, product(): jnp.dot(matrix, vector, preferred_element_type=jnp.float32, precision=lax...  51.3 us
    all_gather x3, blocking collectives, assemble(): whole_quarter = lax.all_gather(block, 'tile', axis=0, tiled=True)  38.3 us
    reduce_scatter x1, waiting for transfers between devices, local(): lax.psum_scatter(product(selector, update), 'tile', scatter_dimension=0,...  35.3 us
  transfers between devices with their start and end apart: 13, of which 13 were waited for; matrix products, arithmetic and copies ran while one was open for 0% of the time, Pallas kernels for 0%

commit v1 on v0

v1 whole, which is shorter than its diff:
```python
import functools

import jax
import jax.numpy as jnp
from jax import lax
from jax.experimental import pallas as pl
from jax.experimental.pallas import tpu as pltpu
from jax.sharding import PartitionSpec as P

F32 = jnp.float32
BF16 = jnp.bfloat16


def split(x):
    high = x.astype(BF16)
    return high, (x - high.astype(F32)).astype(BF16)


def dot(a, b):
    return jnp.dot(a, b, preferred_element_type=F32)


def dot3(a, b):
    ah, al = a
    bh, bl = b
    return dot(ah, bh) + (dot(ah, bl) + dot(al, bh))


def cut_rows(rows, parts):
    units = rows // 8
    sizes = [8 * (units // parts + (1 if p < units % parts else 0)) for p in range(parts)]
    starts = [sum(sizes[:p]) for p in range(parts)]
    return list(zip(starts, sizes))


def rotate(items, by):
    by %= len(items)
    return items[by:] + items[:by]


def kernel(
    tile_bits,
    rhs_hbm, lower_hbm, border_hbm, ub_hbm, upper_hbm, prhs_ref, plower_hbm, pupper_hbm,
    map_ref, count_ref,
    child_out, parent_out,
    rhs_buf, fc_buf, red_buf, p1, p2, p3, part, landing,
    lower, border, ub, upper, plower, pupper, ub_high, ub_low, ubp_high, ubp_low,
    send_sems, recv_sems, load_sems,
):
    tile = lax.axis_index("tile")
    front = lax.axis_index("front")
    rows, width = child_out.shape
    slab = prhs_ref.shape[0]
    parent_rows = plower.shape[1]
    border_total = ub.shape[1]
    border_own = border.shape[0]
    quarter_rows = parent_rows // 4

    def bit_of(axis, b):
        return ((tile if axis == "tile" else front) // (1 << b)) % 2

    def partner(axis, b):
        pos = tile if axis == "tile" else front
        return {axis: pos + (1 << b) * (1 - 2 * bit_of(axis, b))}

    child_dims = [("tile", b) for b in reversed(range(tile_bits))]
    parent_dims = [("front", 1), ("front", 0)] + child_dims

    loads = []
    pairs = (
        (rhs_hbm, rhs_buf.at[tuple(bit_of(*d) for d in child_dims)]),
        (ub_hbm, ub), (lower_hbm, lower), (border_hbm, border),
        (plower_hbm, plower), (pupper_hbm, pupper), (upper_hbm, upper),
    )
    for i, (src, dst) in enumerate(pairs):
        load = pltpu.make_async_copy(src, dst, load_sems.at[i])
        load.start()
        loads.append(load)

    barrier = pltpu.get_barrier_semaphore()
    for d in parent_dims:
        pl.semaphore_signal(
            barrier, inc=1, device_id=partner(*d), device_id_type=pl.DeviceIdType.MESH
        )
    pl.semaphore_wait(barrier, len(parent_dims))

    counter = [0]
    pending = []

    def send(src, dst, d):
        number = counter[0]
        counter[0] += 1
        copy = pltpu.make_async_remote_copy(
            src_ref=src, dst_ref=dst,
            send_sem=send_sems.at[number], recv_sem=recv_sems.at[number],
            device_id=partner(*d), device_id_type=pl.DeviceIdType.MESH,
        )
        copy.start()
        pending.append(copy)
        return copy

    def gather(buf, dims, orders, pieces, fill=None):
        last = [None] * len(pieces)
        held = [set() for _ in pieces]
        for step in range(len(dims)):
            for p, (start, size) in enumerate(pieces):
                if last[p] is not None:
                    last[p].wait_recv()
                d = orders[p][step]
                where = tuple(slice(None) if e in held[p] else bit_of(*e) for e in dims)
                view = buf.at[where + (pl.ds(start, size), slice(None))]
                last[p] = send(view, view, d)
                held[p].add(d)
            if fill is not None:
                fill(step)
        for copy in last:
            copy.wait_recv()

    child_pieces = cut_rows(rows, 2)
    child_orders = [rotate(child_dims[::-1], p * (tile_bits // 2)) for p in range(2)]
    parent_pieces = cut_rows(slab, 3)
    across = [d for d in parent_dims if d != ("front", 0)]
    rotated = [rotate(across, p * len(across) // 3) for p in range(3)]
    parent_orders = [r + [("front", 0)] for r in rotated]
    sum_orders = [[("front", 0)] + r for r in rotated]
    own_child = tuple(bit_of(*d) for d in child_dims)
    own_parent = tuple(bit_of(*d) for d in parent_dims)

    def child_product(matrix, buf, out):
        count = 1 << tile_bits

        def body(j, carry):
            where = tuple((j // (1 << b)) % 2 for _, b in child_dims)
            columns = pl.ds(pl.multiple_of(j * rows, rows), rows)
            term = dot3(split(matrix[:, columns]), split(buf[where]))

            @pl.when(j == 0)
            def _():
                out[...] = term

            @pl.when(j > 0)
            def _():
                out[...] += term

            return carry

        lax.fori_loop(0, count, body, 0)

    def quarter_of(buf, q):
        return buf[q // 2, q % 2].reshape(quarter_rows, width)

    def parent_product(matrix, buf):
        total = None
        for q in range(4):
            columns = slice(q * quarter_rows, (q + 1) * quarter_rows)
            term = dot3(split(matrix[:, columns]), split(quarter_of(buf, q)))
            total = term if total is None else total + term
        return total

    live = count_ref[0]
    chunk = 256
    chunks = parent_rows // chunk

    def permute_chunk(c):
        base = c * chunk
        lanes = lax.broadcasted_iota(jnp.int32, (1, border_total), 1)
        target = jnp.where(lanes < live, map_ref[...], -1) - base
        ids = lax.broadcasted_iota(jnp.int32, (chunk, border_total), 0)
        chosen = jnp.where(ids == target, 1.0, 0.0).astype(BF16)
        columns = pl.ds(pl.multiple_of(base, chunk), chunk)
        over = (((1,), (1,)), ((), ()))
        for source, result in ((ub_high, ubp_high), (ub_low, ubp_low)):
            result[:, columns] = lax.dot_general(
                source[...], chosen, over, preferred_element_type=F32
            ).astype(BF16)

    def permute(step):
        if step == 0:
            loads[1].wait()

            def body(i, carry):
                where = pl.ds(pl.multiple_of(i * 32, 32), 32)
                high, low = split(ub[where, :])
                ub_high[where, :] = high
                ub_low[where, :] = low
                return carry

            lax.fori_loop(0, rows // 32, body, 0)
        low = chunks * step // tile_bits
        top = chunks * (step + 1) // tile_bits

        def body(c, carry):
            permute_chunk(c)
            return carry

        lax.fori_loop(low, top, body, 0)

    loads[0].wait()
    gather(rhs_buf, child_dims, child_orders, child_pieces, permute)
    loads[2].wait()
    own_fc = fc_buf.at[own_child]
    child_product(lower, rhs_buf, own_fc)
    gather(fc_buf, child_dims, child_orders, child_pieces)
    loads[3].wait()
    child_product(border, fc_buf, child_out)

    start = pl.multiple_of(tile * border_own, border_own)
    lanes = start + lax.broadcasted_iota(jnp.int32, (1, border_own), 1)
    target = jnp.where(lanes < live, map_ref[:, pl.ds(start, border_own)], -1)
    high, low = split(child_out[...])
    for q in range(4):
        ids = q * quarter_rows + lax.broadcasted_iota(jnp.int32, (quarter_rows, border_own), 0)
        chosen = jnp.where(ids == target, 1.0, 0.0).astype(BF16)
        block = dot(chosen, high) + dot(chosen, low)
        part[q // 2, q % 2] = block.reshape(part.shape[2:])

    last = [None] * 3
    settled = [[] for _ in range(3)]

    def add_arrived(step, p):
        begin, size = parent_pieces[p]
        last[p].wait_recv()
        where = tuple(bit_of(*e) if e in settled[p] else slice(None) for e in parent_dims)
        where += (pl.ds(begin, size), slice(None))
        part[where] = part[where] + landing[(step,) + where]

    for step in range(len(parent_dims)):
        for p, (begin, size) in enumerate(parent_pieces):
            if step > 0:
                add_arrived(step - 1, p)
            d = sum_orders[p][step]
            where = tuple(
                bit_of(*e) if e in settled[p] else (1 - bit_of(*e) if e == d else slice(None))
                for e in parent_dims
            ) + (pl.ds(begin, size), slice(None))
            last[p] = send(part.at[where], landing.at[(step,) + where], d)
            settled[p].append(d)
    for p in range(3):
        add_arrived(len(parent_dims) - 1, p)

    p1[own_parent] = prhs_ref[...] - part[own_parent]
    gather(p1, parent_dims, parent_orders, parent_pieces)
    loads[4].wait()
    p2[own_parent] = parent_product(plower, p1)
    gather(p2, parent_dims, parent_orders, parent_pieces)
    loads[5].wait()
    solved = parent_product(pupper, p2)
    p3[own_parent] = solved
    parent_out[...] = solved
    gather(p3, parent_dims, parent_orders, parent_pieces)

    total = own_fc[...]
    for q in range(4):
        columns = slice(q * quarter_rows, (q + 1) * quarter_rows)
        pair = (ubp_high[:, columns], ubp_low[:, columns])
        total = total - dot3(pair, split(quarter_of(p3, q)))
    red_buf[own_child] = total
    gather(red_buf, child_dims, child_orders, child_pieces)
    loads[6].wait()
    child_product(upper, red_buf, child_out)
    for copy in pending:
        copy.wait_send()


def local(
    child_rhs, child_lower, child_border, child_upper_border, child_upper,
    parent_rhs, parent_lower, parent_upper, border_map, border_count,
):
    tiles = lax.axis_size("tile")
    tile_bits = tiles.bit_length() - 1
    rows, width = child_rhs.shape[1:]
    slab = parent_rhs.shape[1]
    child_shape = (2,) * tile_bits + (rows, width)
    parent_shape = (2,) * (tile_bits + 2) + (slab, width)
    steps = tile_bits + 2
    sends = 3 * 2 * tile_bits + 4 * 3 * steps
    vmem = pl.BlockSpec(memory_space=pltpu.VMEM)
    hbm = pl.BlockSpec(memory_space=pl.ANY)
    smem = pl.BlockSpec(memory_space=pltpu.SMEM)
    matrices = [child_lower, child_border, child_upper_border, child_upper, parent_lower, parent_upper]
    child_solution, solved = pl.pallas_call(
        functools.partial(kernel, tile_bits),
        out_shape=(
            jax.ShapeDtypeStruct((rows, width), F32),
            jax.ShapeDtypeStruct((slab, width), F32),
        ),
        in_specs=[hbm, hbm, hbm, hbm, hbm, vmem, hbm, hbm, vmem, smem],
        out_specs=(vmem, vmem),
        scratch_shapes=[pltpu.VMEM(child_shape, F32)] * 3
        + [pltpu.VMEM(parent_shape, F32)] * 4
        + [pltpu.VMEM((steps,) + parent_shape, F32)]
        + [pltpu.VMEM(m.shape[1:], F32) for m in matrices]
        + [pltpu.VMEM(child_upper_border.shape[1:], BF16)] * 2
        + [pltpu.VMEM((rows, parent_lower.shape[2]), BF16)] * 2
        + [
            pltpu.SemaphoreType.DMA((sends,)),
            pltpu.SemaphoreType.DMA((sends,)),
            pltpu.SemaphoreType.DMA((7,)),
        ],
        compiler_params=pltpu.CompilerParams(
            collective_id=0, has_side_effects=True, vmem_limit_bytes=60 << 20
        ),
    )(
        child_rhs[0], child_lower[0], child_border[0], child_upper_border[0], child_upper[0],
        parent_rhs[0], parent_lower[0], parent_upper[0], border_map, border_count,
    )
    return (child_solution[None], solved[None])


def solution(mesh):
    return jax.shard_map(
        local,
        mesh=mesh,
        in_specs=(
            P("front", "tile", None),
            P("front", "tile", None),
            P("front", "tile", None),
            P("front", "tile", None),
            P("front", "tile", None),
            P("front", "tile", None),
            P("front", "tile", None),
            P("front", "tile", None),
            P("front", None),
            P("front"),
        ),
        out_specs=(P("front", "tile", None), P("front", "tile", None)),
        check_vma=False,
    )
```

time: 389 us -> 136 us (0.35)
  waiting for transfers between devices: 265 us -> 0 us
  Pallas kernels: 0 us -> 130 us
  matrix products: 51.3 us -> 0 us
  blocking collectives: 38.3 us -> 0 us
  between operations: 14.7 us -> 1.29 us
  starting transfers between devices: 6.48 us -> 0 us
  local copies, waits for them, and re-layouts: 8.67 us -> 3.44 us
  other arithmetic: 4.29 us -> 0 us
    all_gather x4 -> x0, waiting for transfers between devices: 144 us -> none  [apply_rows(): lax.all_gather(local_rows, 'tile', axis=0, tiled=True)]
    pallas_call x0 -> x1, Pallas kernels: none -> 130 us  [local(): pl.pallas_call(functools.partial(kernel, tile_bits), out_shape=(jax.Shape...]
    ppermute x8 -> x0, waiting for transfers between devices: 84.6 us -> none  [partner_2(): return lax.ppermute(block, axis, route)]
    dot_general x8 -> x0, matrix products: 51.3 us -> none  [product(): jnp.dot(matrix, vector, preferred_element_type=jnp.float32, precision=lax...]
    all_gather x3 -> x0, blocking collectives: 38.3 us -> none  [assemble(): whole_quarter = lax.all_gather(block, 'tile', axis=0, tiled=True)]
    reduce_scatter x1 -> x0, waiting for transfers between devices: 35.3 us -> none  [local(): lax.psum_scatter(product(selector, update), 'tile', scatter_dimension=0,...]
    ppermute x8 -> x0, starting transfers between devices: 6.28 us -> none  [partner_2(): return lax.ppermute(block, axis, route)]
    select_n x3 -> x0, local copies, waits for them, and re-layouts: 5.48 us -> none  [pair_quarters(): jnp.where(upper_bit == 0, jnp.concatenate([stacked, partner], 0), jnp.con...]
  transfers between devices with their start and end apart: 13 -> 0, of which waited for: 13 -> 0; matrix products, arithmetic and copies ran while one was open for 0% -> 0% of each run, Pallas kernels for 0% -> 0%
where the time goes in v1:
time: 136 us; the launch traced here: 135 us
  Pallas kernels  130 us (96%)
  local copies, waits for them, and re-layouts  3.44 us (3%)
    pallas_call x1, Pallas kernels, local(): pl.pallas_call(functools.partial(kernel, tile_bits), out_shape=(jax.Shape...  130 us
    unnamed x2, local copies, waits for them, and re-layouts  3.44 us

profile of v1, /device:TPU:0, one launch (start us, length us, event | category | flops | bytes accessed | tf_op | source)
XLA Modules:
  0.0 134.9 jit_solution(13463658747166082330)
XLA Ops:
  1.3 130.2 %shard_map.113 = (f32[512,256]{1,0:T(8,128)}, f32[128,256]{1,0:T(8,128)}) custom-call(f32[512,256]{1,0:T(8,128)} %bitcast.17, f32[512,2048]{1,0:T(8,128)} %bitcast.10, f32[512,2048]{1,0:T(8,128)} %bitcast.11, f32[512,2048]{1,0:T(8,128)} %bitcast.12, f32[512,2048]{1,0:T(8,128)} %bitcast.13, f32[128,256]{1,0:T(8,128)} %bitcast.18, f32[128,2048]{1,0:T(8,128)} %bitcast.14, ...), custom_call_target="tpu_custom_call" | custom-call | tf_op jit(solution)/shard_map/pallas_call | solution.py:281
  131.5 1.9 %copy.15 = f32[1,512,256]{2,1,0:T(8,128)} copy(f32[1,512,256]{2,1,0:T(8,128)} %bitcast.16) | data formatting | bytes 1048576
  133.4 1.6 %copy.16 = f32[1,128,256]{2,1,0:T(8,128)} copy(f32[1,128,256]{2,1,0:T(8,128)} %bitcast.19) | data formatting | bytes 262144

commit v2 on v1

--- a/solution.py
+++ b/solution.py
@@ -116,6 +116,73 @@
         for copy in last:
             copy.wait_recv()
 
+    def flood(buf, dims, orders, pieces):
+        depth = len(dims)
+        paths = [
+            tuple(i for i in range(depth) if m >> i & 1) for m in range(1, 1 << depth)
+        ]
+        copies = {}
+
+        def launch(p, path):
+            start, size = pieces[p]
+            flipped = [orders[p][i] for i in path[:-1]]
+            where = tuple(1 - bit_of(*e) if e in flipped else bit_of(*e) for e in dims)
+            view = buf.at[where + (pl.ds(start, size), slice(None))]
+            copies[p, path] = send(view, view, orders[p][path[-1]])
+
+        def wait(p, path):
+            copies[p, path].wait_recv()
+            for i in range(path[-1] + 1, depth):
+                launch(p, path + (i,))
+
+        for i in range(depth):
+            for p in range(len(pieces)):
+                launch(p, (i,))
+        return paths, wait
+
+    def gather_parent(buf):
+        if tile_bits > 2:
+            gather(buf, parent_dims, parent_orders, parent_pieces)
+            return
+        paths, wait = flood(buf, parent_dims, parent_orders, parent_pieces)
+        for path in sorted(paths, key=lambda path: (len(path), path)):
+            for p in range(3):
+                wait(p, path)
+
+    def apply_child(matrix, buf, out, load, fill=None):
+        if tile_bits > 2:
+            gather(buf, child_dims, child_orders, child_pieces, fill)
+            load.wait()
+            child_product(matrix, buf, out)
+            return
+        paths, wait = flood(buf, child_dims, child_orders, child_pieces)
+
+        def use(flips, first=False):
+            where = tuple(1 - bit_of(*e) if e in flips else bit_of(*e) for e in child_dims)
+            j = sum(w * (1 << b) for w, (_, b) in zip(where, child_dims))
+            columns = pl.ds(pl.multiple_of(j * rows, rows), rows)
+            term = dot3(split(matrix[:, columns]), split(buf[where]))
+            if first:
+                out[...] = term
+            else:
+                out[...] += term
+
+        if fill is not None:
+            fill(0)
+        load.wait()
+        use((), True)
+        wait(0, (0,))
+        wait(1, (0,))
+        if fill is not None:
+            fill(1)
+        wait(0, (1,))
+        wait(1, (1,))
+        use(child_dims[:1])
+        use(child_dims[1:])
+        wait(0, (0, 1))
+        wait(1, (0, 1))
+        use(child_dims)
+
     child_pieces = cut_rows(rows, 2)
     child_orders = [rotate(child_dims[::-1], p * (tile_bits // 2)) for p in range(2)]
     parent_pieces = cut_rows(slab, 3)
@@ -196,26 +263,37 @@
         lax.fori_loop(low, top, body, 0)
 
     loads[0].wait()
-    gather(rhs_buf, child_dims, child_orders, child_pieces, permute)
-    loads[2].wait()
     own_fc = fc_buf.at[own_child]
-    child_product(lower, rhs_buf, own_fc)
-    gather(fc_buf, child_dims, child_orders, child_pieces)
-    loads[3].wait()
-    child_product(border, fc_buf, child_out)
+    apply_child(lower, rhs_buf, own_fc, loads[2], permute)
+    apply_child(border, fc_buf, child_out, loads[3])
 
     start = pl.multiple_of(tile * border_own, border_own)
     lanes = start + lax.broadcasted_iota(jnp.int32, (1, border_own), 1)
     target = jnp.where(lanes < live, map_ref[:, pl.ds(start, border_own)], -1)
     high, low = split(child_out[...])
-    for q in range(4):
+    core = bit_of("front", 0)
+
+    def contributions(high_bit, low_bit):
+        q = high_bit * 2 + low_bit
         ids = q * quarter_rows + lax.broadcasted_iota(jnp.int32, (quarter_rows, border_own), 0)
         chosen = jnp.where(ids == target, 1.0, 0.0).astype(BF16)
         block = dot(chosen, high) + dot(chosen, low)
-        part[q // 2, q % 2] = block.reshape(part.shape[2:])
+        part[high_bit, low_bit] = block.reshape(part.shape[2:])
+
+    handed = []
+    for high_bit in range(2):
+        contributions(high_bit, 1 - core)
+        handed.append(
+            send(part.at[high_bit, 1 - core], landing.at[0, high_bit, 1 - core], ("front", 0))
+        )
+    for high_bit in range(2):
+        contributions(high_bit, core)
+    for high_bit in range(2):
+        handed[high_bit].wait_recv()
+        part[high_bit, core] = part[high_bit, core] + landing[0, high_bit, core]
 
     last = [None] * 3
-    settled = [[] for _ in range(3)]
+    settled = [[("front", 0)] for _ in range(3)]
 
     def add_arrived(step, p):
         begin, size = parent_pieces[p]
@@ -224,9 +302,9 @@
         where += (pl.ds(begin, size), slice(None))
         part[where] = part[where] + landing[(step,) + where]
 
-    for step in range(len(parent_dims)):
+    for step in range(1, len(parent_dims)):
         for p, (begin, size) in enumerate(parent_pieces):
-            if step > 0:
+            if step > 1:
                 add_arrived(step - 1, p)
             d = sum_orders[p][step]
             where = tuple(
@@ -239,15 +317,15 @@
         add_arrived(len(parent_dims) - 1, p)
 
     p1[own_parent] = prhs_ref[...] - part[own_parent]
-    gather(p1, parent_dims, parent_orders, parent_pieces)
+    gather_parent(p1)
     loads[4].wait()
     p2[own_parent] = parent_product(plower, p1)
-    gather(p2, parent_dims, parent_orders, parent_pieces)
+    gather_parent(p2)
     loads[5].wait()
     solved = parent_product(pupper, p2)
     p3[own_parent] = solved
     parent_out[...] = solved
-    gather(p3, parent_dims, parent_orders, parent_pieces)
+    gather_parent(p3)
 
     total = own_fc[...]
     for q in range(4):
@@ -255,9 +333,7 @@
         pair = (ubp_high[:, columns], ubp_low[:, columns])
         total = total - dot3(pair, split(quarter_of(p3, q)))
     red_buf[own_child] = total
-    gather(red_buf, child_dims, child_orders, child_pieces)
-    loads[6].wait()
-    child_product(upper, red_buf, child_out)
+    apply_child(upper, red_buf, child_out, loads[6])
     for copy in pending:
         copy.wait_send()
 
@@ -274,6 +350,8 @@
     parent_shape = (2,) * (tile_bits + 2) + (slab, width)
     steps = tile_bits + 2
     sends = 3 * 2 * tile_bits + 4 * 3 * steps
+    if tile_bits <= 2:
+        sends = 3 * 2 * (tiles - 1) + 3 * 3 * (4 * tiles - 1) + 3 * steps
     vmem = pl.BlockSpec(memory_space=pltpu.VMEM)
     hbm = pl.BlockSpec(memory_space=pl.ANY)
     smem = pl.BlockSpec(memory_space=pltpu.SMEM)

time: 136 us -> 124 us (0.912)
  Pallas kernels: 130 us -> 119 us
    pallas_call x1, Pallas kernels: 130 us -> 119 us  [local(): pl.pallas_call(functools.partial(kernel, tile_bits), out_shape=(jax.Shape...]
where the time goes in v2:
time: 124 us
  Pallas kernels  119 us (96%)
  local copies, waits for them, and re-layouts  3.44 us (3%)
  between operations  1.29 us (1%)
    pallas_call x1, Pallas kernels, local(): pl.pallas_call(functools.partial(kernel, tile_bits), out_shape=(jax.Shape...  119 us
    unnamed x2, local copies, waits for them, and re-layouts  3.44 us

profile of v2, /device:TPU:0, one launch (start us, length us, event | category | flops | bytes accessed | tf_op | source)
XLA Modules:
  0.0 123.6 jit_solution(3085380650628294734)
XLA Ops:
  1.3 118.9 %shard_map.113 = (f32[512,256]{1,0:T(8,128)}, f32[128,256]{1,0:T(8,128)}) custom-call(f32[512,256]{1,0:T(8,128)} %bitcast.17, f32[512,2048]{1,0:T(8,128)} %bitcast.10, f32[512,2048]{1,0:T(8,128)} %bitcast.11, f32[512,2048]{1,0:T(8,128)} %bitcast.12, f32[512,2048]{1,0:T(8,128)} %bitcast.13, f32[128,256]{1,0:T(8,128)} %bitcast.18, f32[128,2048]{1,0:T(8,128)} %bitcast.14, ...), custom_call_target="tpu_custom_call" | custom-call | tf_op jit(solution)/shard_map/pallas_call | solution.py:359
  120.1 1.9 %copy.15 = f32[1,512,256]{2,1,0:T(8,128)} copy(f32[1,512,256]{2,1,0:T(8,128)} %bitcast.16) | data formatting | bytes 1048576
  122.0 1.6 %copy.16 = f32[1,128,256]{2,1,0:T(8,128)} copy(f32[1,128,256]{2,1,0:T(8,128)} %bitcast.19) | data formatting | bytes 262144

commit v3 on v2

--- a/solution.py
+++ b/solution.py
@@ -40,11 +40,12 @@
 
 def kernel(
     tile_bits,
-    rhs_hbm, lower_hbm, border_hbm, ub_hbm, upper_hbm, prhs_ref, plower_hbm, pupper_hbm,
-    map_ref, count_ref,
-    child_out, parent_out,
+    rhs_hbm, lower_hbm, border_hbm, ub_hbm, upper_hbm, prhs_hbm, plower_hbm, pupper_hbm,
+    map_hbm, count_hbm,
+    child_out, parent_hbm,
     rhs_buf, fc_buf, red_buf, p1, p2, p3, part, landing,
     lower, border, ub, upper, plower, pupper, ub_high, ub_low, ubp_high, ubp_low,
+    prhs_ref, map_ref, count_ref, parent_out,
     send_sems, recv_sems, load_sems,
 ):
     tile = lax.axis_index("tile")
@@ -71,11 +72,12 @@
         (rhs_hbm, rhs_buf.at[tuple(bit_of(*d) for d in child_dims)]),
         (ub_hbm, ub), (lower_hbm, lower), (border_hbm, border),
         (plower_hbm, plower), (pupper_hbm, pupper), (upper_hbm, upper),
+        (map_hbm, map_ref), (count_hbm, count_ref), (prhs_hbm, prhs_ref),
     )
     for i, (src, dst) in enumerate(pairs):
         load = pltpu.make_async_copy(src, dst, load_sems.at[i])
-        load.start()
         loads.append(load)
+    loads[0].start()
 
     barrier = pltpu.get_barrier_semaphore()
     for d in parent_dims:
@@ -189,7 +191,8 @@
     across = [d for d in parent_dims if d != ("front", 0)]
     rotated = [rotate(across, p * len(across) // 3) for p in range(3)]
     parent_orders = [r + [("front", 0)] for r in rotated]
-    sum_orders = [[("front", 0)] + r for r in rotated]
+    sum_pieces = cut_rows(slab, 6 if tile_bits <= 2 else 3)
+    sum_orders = [[("front", 0)] + rotated[p % 3] for p in range(len(sum_pieces))]
     own_child = tuple(bit_of(*d) for d in child_dims)
     own_parent = tuple(bit_of(*d) for d in parent_dims)
 
@@ -224,14 +227,13 @@
             total = term if total is None else total + term
         return total
 
-    live = count_ref[0]
     chunk = 256
     chunks = parent_rows // chunk
 
     def permute_chunk(c):
         base = c * chunk
         lanes = lax.broadcasted_iota(jnp.int32, (1, border_total), 1)
-        target = jnp.where(lanes < live, map_ref[...], -1) - base
+        target = jnp.where(lanes < count_ref[0], map_ref[...], -1) - base
         ids = lax.broadcasted_iota(jnp.int32, (chunk, border_total), 0)
         chosen = jnp.where(ids == target, 1.0, 0.0).astype(BF16)
         columns = pl.ds(pl.multiple_of(base, chunk), chunk)
@@ -241,9 +243,16 @@
                 source[...], chosen, over, preferred_element_type=F32
             ).astype(BF16)
 
-    def permute(step):
-        if step == 0:
-            loads[1].wait()
+    shares = ((0, 1, 2), (2, 5, 8))
+
+    def permute(turn, step):
+        if step > 1:
+            return
+        if turn == 0 and step == 0:
+            for i in (7, 8, 2, 1, 3, 9, 4, 5, 6):
+                loads[i].start()
+            for i in (7, 8, 1):
+                loads[i].wait()
 
             def body(i, carry):
                 where = pl.ds(pl.multiple_of(i * 32, 32), 32)
@@ -253,8 +262,8 @@
                 return carry
 
             lax.fori_loop(0, rows // 32, body, 0)
-        low = chunks * step // tile_bits
-        top = chunks * (step + 1) // tile_bits
+        low = chunks * shares[turn][step] // 8
+        top = chunks * shares[turn][step + 1] // 8
 
         def body(c, carry):
             permute_chunk(c)
@@ -264,12 +273,12 @@
 
     loads[0].wait()
     own_fc = fc_buf.at[own_child]
-    apply_child(lower, rhs_buf, own_fc, loads[2], permute)
-    apply_child(border, fc_buf, child_out, loads[3])
+    apply_child(lower, rhs_buf, own_fc, loads[2], functools.partial(permute, 0))
+    apply_child(border, fc_buf, child_out, loads[3], functools.partial(permute, 1))
 
     start = pl.multiple_of(tile * border_own, border_own)
     lanes = start + lax.broadcasted_iota(jnp.int32, (1, border_own), 1)
-    target = jnp.where(lanes < live, map_ref[:, pl.ds(start, border_own)], -1)
+    target = jnp.where(lanes < count_ref[0], map_ref[:, pl.ds(start, border_own)], -1)
     high, low = split(child_out[...])
     core = bit_of("front", 0)
 
@@ -280,30 +289,31 @@
         block = dot(chosen, high) + dot(chosen, low)
         part[high_bit, low_bit] = block.reshape(part.shape[2:])
 
+    far = 1 - bit_of("front", 1)
     handed = []
-    for high_bit in range(2):
+    for high_bit in (far, 1 - far):
         contributions(high_bit, 1 - core)
         handed.append(
             send(part.at[high_bit, 1 - core], landing.at[0, high_bit, 1 - core], ("front", 0))
         )
-    for high_bit in range(2):
+    for high_bit in (far, 1 - far):
         contributions(high_bit, core)
-    for high_bit in range(2):
-        handed[high_bit].wait_recv()
+    for copy, high_bit in zip(handed, (far, 1 - far)):
+        copy.wait_recv()
         part[high_bit, core] = part[high_bit, core] + landing[0, high_bit, core]
 
-    last = [None] * 3
-    settled = [[("front", 0)] for _ in range(3)]
+    last = [None] * len(sum_pieces)
+    settled = [[("front", 0)] for _ in sum_pieces]
 
     def add_arrived(step, p):
-        begin, size = parent_pieces[p]
+        begin, size = sum_pieces[p]
         last[p].wait_recv()
         where = tuple(bit_of(*e) if e in settled[p] else slice(None) for e in parent_dims)
         where += (pl.ds(begin, size), slice(None))
         part[where] = part[where] + landing[(step,) + where]
 
     for step in range(1, len(parent_dims)):
-        for p, (begin, size) in enumerate(parent_pieces):
+        for p, (begin, size) in enumerate(sum_pieces):
             if step > 1:
                 add_arrived(step - 1, p)
             d = sum_orders[p][step]
@@ -313,9 +323,10 @@
             ) + (pl.ds(begin, size), slice(None))
             last[p] = send(part.at[where], landing.at[(step,) + where], d)
             settled[p].append(d)
-    for p in range(3):
+    for p in range(len(sum_pieces)):
         add_arrived(len(parent_dims) - 1, p)
 
+    loads[9].wait()
     p1[own_parent] = prhs_ref[...] - part[own_parent]
     gather_parent(p1)
     loads[4].wait()
@@ -325,7 +336,10 @@
     solved = parent_product(pupper, p2)
     p3[own_parent] = solved
     parent_out[...] = solved
+    leaving = pltpu.make_async_copy(parent_out, parent_hbm, load_sems.at[10])
+    leaving.start()
     gather_parent(p3)
+    leaving.wait()
 
     total = own_fc[...]
     for q in range(4):
@@ -351,10 +365,9 @@
     steps = tile_bits + 2
     sends = 3 * 2 * tile_bits + 4 * 3 * steps
     if tile_bits <= 2:
-        sends = 3 * 2 * (tiles - 1) + 3 * 3 * (4 * tiles - 1) + 3 * steps
+        sends = 3 * 2 * (tiles - 1) + 3 * 3 * (4 * tiles - 1) + 6 * steps
     vmem = pl.BlockSpec(memory_space=pltpu.VMEM)
     hbm = pl.BlockSpec(memory_space=pl.ANY)
-    smem = pl.BlockSpec(memory_space=pltpu.SMEM)
     matrices = [child_lower, child_border, child_upper_border, child_upper, parent_lower, parent_upper]
     child_solution, solved = pl.pallas_call(
         functools.partial(kernel, tile_bits),
@@ -362,8 +375,8 @@
             jax.ShapeDtypeStruct((rows, width), F32),
             jax.ShapeDtypeStruct((slab, width), F32),
         ),
-        in_specs=[hbm, hbm, hbm, hbm, hbm, vmem, hbm, hbm, vmem, smem],
-        out_specs=(vmem, vmem),
+        in_specs=[hbm] * 10,
+        out_specs=(vmem, hbm),
         scratch_shapes=[pltpu.VMEM(child_shape, F32)] * 3
         + [pltpu.VMEM(parent_shape, F32)] * 4
         + [pltpu.VMEM((steps,) + parent_shape, F32)]
@@ -371,9 +384,13 @@
         + [pltpu.VMEM(child_upper_border.shape[1:], BF16)] * 2
         + [pltpu.VMEM((rows, parent_lower.shape[2]), BF16)] * 2
         + [
+            pltpu.VMEM((slab, width), F32),
+            pltpu.VMEM(border_map.shape, jnp.int32),
+            pltpu.SMEM(border_count.shape, jnp.int32),
+            pltpu.VMEM((slab, width), F32),
             pltpu.SemaphoreType.DMA((sends,)),
             pltpu.SemaphoreType.DMA((sends,)),
-            pltpu.SemaphoreType.DMA((7,)),
+            pltpu.SemaphoreType.DMA((11,)),
         ],
         compiler_params=pltpu.CompilerParams(
             collective_id=0, has_side_effects=True, vmem_limit_bytes=60 << 20

time: 124 us -> 121 us (0.976)
  Pallas kernels: 119 us -> 116 us
    pallas_call x1, Pallas kernels: 119 us -> 116 us  [local(): pl.pallas_call(functools.partial(kernel, tile_bits), out_shape=(jax.Shape...]
where the time goes in v3:
time: 121 us
  Pallas kernels  116 us (96%)
  local copies, waits for them, and re-layouts  3.44 us (3%)
  between operations  1.29 us (1%)
    pallas_call x1, Pallas kernels, local(): pl.pallas_call(functools.partial(kernel, tile_bits), out_shape=(jax.Shape...  116 us
    unnamed x2, local copies, waits for them, and re-layouts  3.44 us

profile of v3, /device:TPU:0, one launch (start us, length us, event | category | flops | bytes accessed | tf_op | source)
XLA Modules:
  0.0 121.0 jit_solution(3184690940864572603)
XLA Ops:
  1.3 116.3 %shard_map.113 = (f32[512,256]{1,0:T(8,128)}, f32[128,256]{1,0:T(8,128)}) custom-call(f32[512,256]{1,0:T(8,128)} %bitcast.17, f32[512,2048]{1,0:T(8,128)} %bitcast.10, f32[512,2048]{1,0:T(8,128)} %bitcast.11, f32[512,2048]{1,0:T(8,128)} %bitcast.12, f32[512,2048]{1,0:T(8,128)} %bitcast.13, f32[128,256]{1,0:T(8,128)} %bitcast.18, f32[128,2048]{1,0:T(8,128)} %bitcast.14, ...), custom_call_target="tpu_custom_call" | custom-call | tf_op jit(solution)/shard_map/pallas_call | solution.py:372
  117.6 1.9 %copy.15 = f32[1,512,256]{2,1,0:T(8,128)} copy(f32[1,512,256]{2,1,0:T(8,128)} %bitcast.16) | data formatting | bytes 1048576
  119.5 1.6 %copy.16 = f32[1,128,256]{2,1,0:T(8,128)} copy(f32[1,128,256]{2,1,0:T(8,128)} %bitcast.19) | data formatting | bytes 262144
